TPU v7x, 128 devices: a whole 4x4x4 slice. The times are simulated.
128 devices in a mesh: pair: 2 (over core), row: 64 (over z, y, x).
Axes of the slice: x: 4, y: 4, z: 4, core: 2. Of those that a mesh axis runs over, the one named last changes fastest.
Arguments:
- snapshot: float32 [16384, 1024], P('row', 'pair'), may hold values from -6 to 6
- weights: float32 [8, 128], replicated, may hold values from 0 to 1
- block_home: int32 [8], P('pair'), may hold values from 0 to 7, each once
- plan: int32 [2, 2, 4], P(None, 'pair'), may hold values from 0 to 3, each once within a row
Outputs:
- rotated: float32 [16384, 1024], P('row', 'pair')
- column_norms: float32 [1024], P('pair')
All inputs are finite; a program needn't handle non-finite values. Where the computation divides by a largest or mean magnitude, that divisor is 1e-20 or more.
Results may differ from a plain program's by a relative error of at most 0.0001.
Values sent between devices are 32-bit elements; how exact they have to be, the bound alone decides.
A program may use at most 128 MiB of HBM per device.

v0:
```python
import jax
import jax.numpy as jnp
from jax import lax
from jax.sharding import PartitionSpec as P

epsilon = 1e-06
step_size = 4.0
newton_turns = 5
highest = lax.Precision.HIGHEST


def split_up(value, dim, length):
    before, after = (value.shape[:dim], value.shape[dim + 1 :])
    return jnp.moveaxis(value.reshape(*before, length, -1, *after), dim, 0)


def summed_on_arrival(value, axis, dim):
    length = lax.axis_size(axis)
    blocks = lax.all_to_all(split_up(value, dim, length), axis, 0, 0, tiled=True)
    return jnp.sum(blocks, axis=0)


def filled_up(lines, length):
    spare = -lines.shape[0] % length
    if not spare:
        return lines
    return jnp.concatenate([lines, jnp.zeros((spare, *lines.shape[1:]), lines.dtype)])


def copy_for_each(value, axis):
    copies = jnp.broadcast_to(value, (lax.axis_size(axis), *value.shape))
    return lax.all_to_all(copies, axis, split_axis=0, concat_axis=0, tiled=True)


def joined_along(blocks, dim):
    blocks = jnp.moveaxis(blocks, 0, dim)
    shape = blocks.shape
    return blocks.reshape(*shape[:dim], shape[dim] * shape[dim + 1], *shape[dim + 2 :])


def gathered_copies(value, axis, dim):
    blocks = copy_for_each(value, axis)
    return joined_along(blocks, dim)


def sum_by_parts(value, axes):
    lines = value.reshape(-1, value.shape[-1])
    own = summed_on_arrival(filled_up(lines, lax.axis_size(axes)), axes, 0)
    whole = gathered_copies(own, axes, 0)
    return whole[: len(lines)].reshape(value.shape)


def shifted(block, axis, distance):
    devices = range(lax.axis_size(axis))
    route = [((i - distance) % len(devices), i) for i in devices]
    return lax.ppermute(block, axis, route)


def over_copies(value, axis):
    everything = copy_for_each(value, axis)
    return jnp.sum(everything, axis=0)


def rotation(gram_matrix, spread):
    diagonal_part = jnp.diagonal(gram_matrix, axis1=1, axis2=2)
    inverse = lax.rsqrt(diagonal_part + epsilon)
    corr = gram_matrix * inverse[:, :, None] * inverse[:, None, :]
    skew_part = step_size * corr * (spread[:, :, None] - spread[:, None, :])
    row_bound = 1.0 + jnp.max(jnp.sum(jnp.abs(skew_part), axis=2), axis=1)
    unit_matrix = jnp.eye(gram_matrix.shape[1], dtype=jnp.float32)
    current = unit_matrix[None] + skew_part / row_bound[:, None, None]
    for index in range(newton_turns):
        inner_gram = jnp.einsum("pcd,pce->pde", current, current, precision=highest)
        current = jnp.einsum(
            "pcd,pde->pce", current, 1.5 * unit_matrix[None] - 0.5 * inner_gram, precision=highest
        )
    return current


def full_gram(paired):
    local_gram = jnp.einsum("rpc,rpd->pcd", paired, paired, precision=highest)
    return sum_by_parts(local_gram, "row")


def body(snapshot, weights, block_home, plan):
    row_count = snapshot.shape[0]
    block_width = weights.shape[1]
    slot_count = block_home.shape[0]
    rounds = plan.shape[0]
    blocks_here = snapshot.reshape(row_count, slot_count, block_width)
    spread = jnp.take(weights, block_home, axis=0)
    for round_index in range(rounds):
        ordering = plan[round_index, 0]
        blocks_here = jnp.take(blocks_here, ordering, axis=1)
        spread = jnp.take(spread, ordering, axis=0)
        paired = blocks_here.reshape(row_count, 2, 2 * block_width)
        gram_matrix = full_gram(paired)
        turn_matrix = rotation(gram_matrix, spread.reshape(2, 2 * block_width))
        result = jnp.einsum("rpc,pcd->rpd", paired, turn_matrix, precision=highest)
        blocks_here = result.reshape(row_count, slot_count, block_width)
        ahead_block, ahead_scale = shifted((blocks_here[:, 0], spread[0]), "pair", 1)
        behind_block, behind_scale = shifted((blocks_here[:, 3], spread[3]), "pair", -1)
        blocks_here = jnp.stack(
            [ahead_block, blocks_here[:, 1], blocks_here[:, 2], behind_block], axis=1
        )
        spread = jnp.stack([ahead_scale, spread[1], spread[2], behind_scale], axis=0)
    final_matrix = blocks_here.reshape(row_count, slot_count * block_width)
    squares = over_copies(jnp.sum(final_matrix * final_matrix, axis=0), "row")
    return (final_matrix, jnp.sqrt(squares))


def solution(mesh):
    in_specs = (P("row", "pair"), P(), P("pair"), P(None, "pair", None))
    out_specs = (P("row", "pair"), P("pair"))
    return jax.shard_map(body, mesh=mesh, in_specs=in_specs, out_specs=out_specs, check_vma=False)
```

profile of v0, /device:TPU:1, one launch (start us, length us, event | category | flops | bytes accessed | tf_op | source)
XLA Modules:
  0.0 164.7 jit_solution(13016233021426600878)
XLA Ops:
  0.6 0.7 compare_and_fusion
  1.3 1.2 copy.93
  3.7 1.5 fusion.12
  5.2 12.0 %all-to-all-start = ((f32[64,8,256]{2,1,0:T(8,128)}), f32[64,8,256]{2,1,0:T(8,128)S(1)}, u32[]{:S(2)}, u32[]{:S(2)}) async-start(f32[64,8,256]{2,1,0:T(8,128)} %bitcast.5), calls=%async_computation | async-start | bytes 1048576 | tf_op jit(solution)/shard_map/all_to_all | solution.py:19
  17.1 0.7 compare_select_fusion.2
  18.4 0.7 compare_and_fusion.2
  19.7 9.6 %all-to-all-done = f32[64,8,256]{2,1,0:T(8,128)S(1)} async-done(((f32[64,8,256]{2,1,0:T(8,128)}), f32[64,8,256]{2,1,0:T(8,128)S(1)}, u32[]{:S(2)}, u32[]{:S(2)}) %all-to-all-start) | async-done | bytes 524320 | tf_op jit(solution)/shard_map/all_to_all | solution.py:19
  29.3 0.8 broadcast_in_dim.65
  30.1 4.8 %all-to-all-start.1 = ((f32[64,8,256]{2,1,0:T(8,128)}), f32[64,8,256]{2,1,0:T(8,128)S(1)}, u32[]{:S(2)}, u32[]{:S(2)}) async-start(f32[64,8,256]{2,1,0:T(8,128)} %broadcast_in_dim.65), calls=%async_computation.1 | async-start | bytes 1048576 | tf_op jit(solution)/shard_map/all_to_all | solution.py:32
  35.2 10.7 %all-to-all-done.1 = f32[64,8,256]{2,1,0:T(8,128)S(1)} async-done(((f32[64,8,256]{2,1,0:T(8,128)}), f32[64,8,256]{2,1,0:T(8,128)S(1)}, u32[]{:S(2)}, u32[]{:S(2)}) %all-to-all-start.1) | async-done | bytes 524320 | tf_op jit(solution)/shard_map/all_to_all | solution.py:32
  45.9 16.4 %copy.97 = f32[2,256,256]{0,2,1:T(8,128)} copy(f32[2,256,256]{2,1,0:T(8,128)S(1)} %bitcast.108) | data formatting | bytes 1048576 | tf_op jit(solution)/shard_map/reshape;reshape | solution.py:50
  62.3 2.3 %gather_fusion = f32[256,2]{1,0:T(8,128)S(1)} fusion(f32[2,256,256]{0,2,1:T(8,128)} %copy.97, s32[256]{0:T(256)S(1)} %bitcast.104), kind=kCustom, calls=%fused_computation.4 | custom fusion | bytes 6144 | tf_op jit(solution)/shard_map/jit(diagonal)/gather | solution.py:65
  65.7 1.1 fusion.9
  66.8 0.7 fusion.13
  67.5 1.1 fusion.8
  68.6 0.7 fusion.14
  69.2 1.1 fusion.7
  70.3 0.7 fusion.15
  71.0 1.1 fusion.6
  72.7 1.1 fusion.5
  73.8 1.1 fusion.17
  74.9 0.7 fusion.18
  75.6 3.3 %collective-permute-start = (f32[256,128]{0,1:T(8,128)S(1)}, f32[256,128]{0,1:T(8,128)S(1)}, u32[]{:S(2)}, u32[]{:S(2)}) collective-permute-start(f32[256,128]{0,1:T(8,128)S(1)} %get-tuple-element.12), channel_id=1, source_target_pairs={{64,0},{0,64},{65,1},{1,65},{66,2},{2,66},{67,3},{3,67},{68,4},{4,... | collective-permute-start | bytes 393224 | tf_op jit(solution)/shard_map/ppermute | solution.py:56
  81.0 0.7 fusion.19
  81.6 16.8 %all_to_all.26 = f32[64,8,256]{2,1,0:T(8,128)S(1)} all-to-all(f32[64,8,256]{2,1,0:T(8,128)S(1)} %bitcast.118), channel_id=1, replica_groups=mesh['pair'=2,'row'=64] {'row'}, dimensions={0} | all-to-all | bytes 1048576 | tf_op jit(solution)/shard_map/all_to_all | solution.py:19
  98.5 0.8 broadcast_in_dim.69
  99.3 4.6 %all-to-all-start.3 = ((f32[64,8,256]{2,1,0:T(8,128)}), f32[64,8,256]{2,1,0:T(8,128)S(1)}, u32[]{:S(2)}, u32[]{:S(2)}) async-start(f32[64,8,256]{2,1,0:T(8,128)} %broadcast_in_dim.69), calls=%async_computation.3 | async-start | bytes 1048576 | tf_op jit(solution)/shard_map/all_to_all | solution.py:32
  104.0 2.0 %collective-permute-start.2 = (f32[128]{0:T(128)S(1)}, f32[128]{0:T(128)S(1)}, u32[]{:S(2)}, u32[]{:S(2)}) collective-permute-start(f32[128]{0:T(128)S(1)} %get-tuple-element.14), channel_id=1, source_target_pairs={{64,0},{0,64},{65,1},{1,65},{66,2},{2,66},{67,3},{3,67},{68,4},{4,... | collective-permute-start | bytes 1544 | tf_op jit(solution)/shard_map/ppermute | solution.py:56
  106.0 0.7 collective-permute-done.2
  107.8 7.5 %all-to-all-done.3 = f32[64,8,256]{2,1,0:T(8,128)S(1)} async-done(((f32[64,8,256]{2,1,0:T(8,128)}), f32[64,8,256]{2,1,0:T(8,128)S(1)}, u32[]{:S(2)}, u32[]{:S(2)}) %all-to-all-start.3) | async-done | bytes 524320 | tf_op jit(solution)/shard_map/all_to_all | solution.py:32
  115.3 16.4 %copy.111 = f32[2,256,256]{0,2,1:T(8,128)} copy(f32[2,256,256]{2,1,0:T(8,128)S(1)} %bitcast.106) | data formatting | bytes 1048576 | tf_op jit(solution)/shard_map/reshape;reshape | solution.py:50
  131.7 2.3 %gather_fusion.2 = f32[256,2]{1,0:T(8,128)S(1)} fusion(f32[2,256,256]{0,2,1:T(8,128)} %copy.111, s32[256]{0:T(256)S(1)} %bitcast.105), kind=kCustom, calls=%fused_computation.6 | custom fusion | bytes 6144 | tf_op jit(solution)/shard_map/jit(diagonal)/gather | solution.py:65
  135.1 1.1 fusion.4
  136.2 0.7 fusion.20
  136.9 1.1 fusion.3
  138.0 0.7 fusion.21
  138.6 1.1 fusion.2
  140.4 1.1 fusion.1
  141.5 0.7 fusion.23
  142.2 1.1 fusion
  143.2 1.1 fusion.24
  144.3 0.7 fusion.25
  145.0 3.1 %collective-permute-start.4 = (f32[256,128]{0,1:T(8,128)S(1)}, f32[256,128]{0,1:T(8,128)S(1)}, u32[]{:S(2)}, u32[]{:S(2)}) collective-permute-start(f32[256,128]{0,1:T(8,128)S(1)} %get-tuple-element.10), channel_id=1, source_target_pairs={{64,0},{0,64},{65,1},{1,65},{66,2},{2,66},{67,3},{3,67},{68,4},{4,... | collective-permute-start | bytes 393224 | tf_op jit(solution)/shard_map/ppermute | solution.py:56
  148.2 0.9 collective-permute-done.4
  149.6 0.7 broadcast_in_dim.71
  150.3 4.6 %all-to-all-start.4 = ((f32[64,1,512]{2,1,0:T(1,128)}), f32[64,1,512]{2,1,0:T(1,128)S(1)}, u32[]{:S(2)}, u32[]{:S(2)}) async-start(f32[64,1,512]{2,1,0:T(1,128)} %broadcast_in_dim.71), calls=%async_computation.4 | async-start | bytes 262144 | tf_op jit(solution)/shard_map/all_to_all | solution.py:32
  154.9 1.0 copy.142
  155.9 8.1 %all-to-all-done.4 = f32[64,1,512]{2,1,0:T(1,128)S(1)} async-done(((f32[64,1,512]{2,1,0:T(1,128)}), f32[64,1,512]{2,1,0:T(1,128)S(1)}, u32[]{:S(2)}, u32[]{:S(2)}) %all-to-all-start.4) | async-done | bytes 131104 | tf_op jit(solution)/shard_map/all_to_all | solution.py:32
  (70 shorter events, 10.6 us)
Async XLA Ops:
  0.6 17.2 %copy-start = (f32[8,128]{1,0:T(8,128)S(1)}, f32[8,128]{1,0:T(8,128)}, u32[]{:S(2)}) copy-start(f32[8,128]{1,0:T(8,128)} %param.9) | copy-start | bytes 12292
  5.2 24.1 %all-to-all-start = ((f32[64,8,256]{2,1,0:T(8,128)}), f32[64,8,256]{2,1,0:T(8,128)S(1)}, u32[]{:S(2)}, u32[]{:S(2)}) async-start(f32[64,8,256]{2,1,0:T(8,128)} %bitcast.5), calls=%async_computation | async-start | bytes 1048576 | tf_op jit(solution)/shard_map/all_to_all | solution.py:19
  30.1 15.8 %all-to-all-start.1 = ((f32[64,8,256]{2,1,0:T(8,128)}), f32[64,8,256]{2,1,0:T(8,128)S(1)}, u32[]{:S(2)}, u32[]{:S(2)}) async-start(f32[64,8,256]{2,1,0:T(8,128)} %broadcast_in_dim.65), calls=%async_computation.1 | async-start | bytes 1048576 | tf_op jit(solution)/shard_map/all_to_all | solution.py:32
  75.6 4.3 %collective-permute-start = (f32[256,128]{0,1:T(8,128)S(1)}, f32[256,128]{0,1:T(8,128)S(1)}, u32[]{:S(2)}, u32[]{:S(2)}) collective-permute-start(f32[256,128]{0,1:T(8,128)S(1)} %get-tuple-element.12), channel_id=1, source_target_pairs={{64,0},{0,64},{65,1},{1,65},{66,2},{2,66},{67,3},{3,67},{68,4},{4,... | collective-permute-start | bytes 393224 | tf_op jit(solution)/shard_map/ppermute | solution.py:56
  78.9 1.3 collective-permute-start.1
  80.2 84.5 %copy-start.1 = (f32[8,128]{1,0:T(8,128)S(1)}, f32[8,128]{1,0:T(8,128)}, u32[]{:S(2)}) copy-start(f32[8,128]{1,0:T(8,128)} %param.9) | copy-start | bytes 12292
  99.3 16.0 %all-to-all-start.3 = ((f32[64,8,256]{2,1,0:T(8,128)}), f32[64,8,256]{2,1,0:T(8,128)S(1)}, u32[]{:S(2)}, u32[]{:S(2)}) async-start(f32[64,8,256]{2,1,0:T(8,128)} %broadcast_in_dim.69), calls=%async_computation.3 | async-start | bytes 1048576 | tf_op jit(solution)/shard_map/all_to_all | solution.py:32
  104.0 2.8 %collective-permute-start.2 = (f32[128]{0:T(128)S(1)}, f32[128]{0:T(128)S(1)}, u32[]{:S(2)}, u32[]{:S(2)}) collective-permute-start(f32[128]{0:T(128)S(1)} %get-tuple-element.14), channel_id=1, source_target_pairs={{64,0},{0,64},{65,1},{1,65},{66,2},{2,66},{67,3},{3,67},{68,4},{4,... | collective-permute-start | bytes 1544 | tf_op jit(solution)/shard_map/ppermute | solution.py:56
  105.9 1.1 collective-permute-start.3
  145.0 4.1 %collective-permute-start.4 = (f32[256,128]{0,1:T(8,128)S(1)}, f32[256,128]{0,1:T(8,128)S(1)}, u32[]{:S(2)}, u32[]{:S(2)}) collective-permute-start(f32[256,128]{0,1:T(8,128)S(1)} %get-tuple-element.10), channel_id=1, source_target_pairs={{64,0},{0,64},{65,1},{1,65},{66,2},{2,66},{67,3},{3,67},{68,4},{4,... | collective-permute-start | bytes 393224 | tf_op jit(solution)/shard_map/ppermute | solution.py:56
  148.1 1.3 collective-permute-start.5
  150.3 13.7 %all-to-all-start.4 = ((f32[64,1,512]{2,1,0:T(1,128)}), f32[64,1,512]{2,1,0:T(1,128)S(1)}, u32[]{:S(2)}, u32[]{:S(2)}) async-start(f32[64,1,512]{2,1,0:T(1,128)} %broadcast_in_dim.71), calls=%async_computation.4 | async-start | bytes 262144 | tf_op jit(solution)/shard_map/all_to_all | solution.py:32
where the time goes:
time: 165 us
  local copies, waits for them, and re-layouts  46.7 us (28%)
  waiting for transfers between devices  39.1 us (24%)
  starting transfers between devices  34.8 us (21%)
  matrix products  21.7 us (13%)
  blocking collectives  16.8 us (10%)
  other arithmetic  4.49 us (3%)
    another operation x2, local copies, waits for them, and re-layouts, sum_by_parts(): return whole[:len(lines)].reshape(value.shape)  32.8 us
    all_to_all x3, waiting for transfers between devices, copy_for_each(): return lax.all_to_all(copies, axis, split_axis=0, concat_axis=0, tiled=True)  26.2 us
    all_to_all x1, blocking collectives, summed_on_arrival(): lax.all_to_all(split_up(value, dim, length), axis, 0, 0, tiled=True)  16.8 us
    all_to_all x3, starting transfers between devices, copy_for_each(): return lax.all_to_all(copies, axis, split_axis=0, concat_axis=0, tiled=True)  14.1 us
    all_to_all x1, starting transfers between devices, summed_on_arrival(): lax.all_to_all(split_up(value, dim, length), axis, 0, 0, tiled=True)  12 us
    dot_general x10, matrix products, rotation(): inner_gram = jnp.einsum('pcd,pce->pde', current, current, precision=highest)  10.8 us
    all_to_all x1, waiting for transfers between devices, summed_on_arrival(): lax.all_to_all(split_up(value, dim, length), axis, 0, 0, tiled=True)  9.56 us
    ppermute x6, starting transfers between devices, shifted(): return lax.ppermute(block, axis, route)  8.81 us
  transfers between devices with their start and end apart: 10, of which 10 were waited for; matrix products, arithmetic and copies ran while one was open for 3% of the time, Pallas kernels for 0%

commit v1 on v0

v1 whole, which is shorter than its diff:
```python
import functools

import jax
import jax.numpy as jnp
from jax import lax
from jax.experimental import pallas as pl
from jax.experimental.pallas import tpu as pltpu
from jax.sharding import PartitionSpec as P

MESH = pl.DeviceIdType.MESH
f32, bf16 = jnp.float32, jnp.bfloat16
epsilon = 1e-06
step_size = 4.0
B = 128
W = 2 * B
ROWS = 256
SIDE = 4
N = SIDE**3
T = 8
FAR_FIRST = (2, 1, 3, 0)


def split(x):
    hi = x.astype(bf16)
    return hi, (x - hi.astype(f32)).astype(bf16)


def dot(a, b):
    return jnp.dot(a, b, preferred_element_type=f32)


def dot_t(a, b):
    return lax.dot_general(a, b, (((0,), (0,)), ((), ())), preferred_element_type=f32)


def mm(a, b):
    (ah, al), (bh, bl) = a, b
    return dot(jnp.concatenate([ah, ah, al], axis=1), jnp.concatenate([bh, bl, bh], axis=0))


def mm_t(a, b):
    (ah, al), (bh, bl) = a, b
    return dot_t(jnp.concatenate([ah, ah, al], axis=0), jnp.concatenate([bh, bl, bh], axis=0))


def iotas(n):
    return lax.broadcasted_iota(jnp.int32, (n, n), 0), lax.broadcasted_iota(jnp.int32, (n, n), 1)


def eye_mask():
    r, c = iotas(B)
    return r == c


def diag_row(block, eye):
    return jnp.sum(jnp.where(eye, block, 0.0), axis=0, keepdims=True)


def diag_col(block, eye):
    return jnp.sum(jnp.where(eye, block, 0.0), axis=1, keepdims=True)


def weight_steps(w0, w1):
    eye = eye_mask()
    col = jnp.concatenate([diag_col(jnp.broadcast_to(w, (B, B)), eye) for w in (w0, w1)], axis=0)
    row = jnp.concatenate([w0, w1], axis=1)
    return step_size * (col - row)


def generator(gram, steps):
    eye = eye_mask()
    blocks = (gram[:B, :B], gram[B:, B:])
    inv_row = lax.rsqrt(jnp.concatenate([diag_row(b, eye) for b in blocks], axis=1) + epsilon)
    inv_col = lax.rsqrt(jnp.concatenate([diag_col(b, eye) for b in blocks], axis=0) + epsilon)
    skew = (gram * inv_col * inv_row) * steps
    bound = 1.0 + jnp.max(jnp.sum(jnp.abs(skew), axis=0, keepdims=True), axis=1, keepdims=True)
    return skew * (1.0 / bound)


def newton_schulz(gens, between=()):
    r, c = iotas(W)
    unit = (r == c).astype(f32)
    both = range(len(gens))
    s = [split(g) for g in gens]
    z = [-mm(s[h], s[h]) for h in both]
    x = [unit + gens[h] for h in both]
    for k in range(3):
        zs = [split(z[h]) for h in both]
        u = [mm(zs[h], zs[h]) for h in both]
        x = [x[h] - 0.5 * mm(split(x[h]), zs[h]) for h in both]
        z = [-0.75 * u[h] + 0.25 * mm(split(u[h]), zs[h]) for h in both]
        if k < len(between):
            between[k]()
    zs = [split(z[h]) for h in both]
    u = [mm(zs[h], zs[h]) for h in both]
    tail = [split(0.375 * unit - 0.3125 * z[h] + 0.0625 * u[h]) for h in both]
    last = [mm(split(u[h]), tail[h]) - 0.5 * z[h] for h in both]
    return [x[h] + mm(split(x[h]), split(last[h])) for h in both]


def peers_loop(me, send):
    z, y, x = me // (SIDE * SIDE), lax.rem(me // SIDE, SIDE), lax.rem(me, SIDE)
    slot = 0
    for a in FAR_FIRST:
        for b in FAR_FIRST:
            for c in FAR_FIRST:
                if a or b or c:
                    send(slot, lax.rem(z + a, SIDE) * SIDE * SIDE + lax.rem(y + b, SIDE) * SIDE + lax.rem(x + c, SIDE))
                    slot += 1


def kernel(
    snap, wts, home, plan, out, norms,
    xs, praw, ph, plo, wcur, src0, dsrc, rb0, db0, srcx, rbx, g0, gx, gfull, vbuf, vsend, gd, gdsend,
    rot, obuf, nsend, nrecv, lsem, osem, ssem, rsem, dssem, drsem,
):
    core, me = lax.axis_index("pair"), lax.axis_index("row")
    other = (1 - core, me)
    barrier = pltpu.get_barrier_semaphore()
    loads = [pltpu.make_async_copy(snap.at[:, pl.ds(B * s, B)], xs.at[s], lsem.at[s]) for s in range(4)]
    for load in loads:
        load.start()
    pl.semaphore_signal(barrier, inc=1, device_id=other, device_id_type=MESH)
    peers_loop(me, lambda slot, p: pl.semaphore_signal(barrier, inc=1, device_id=(core, p), device_id_type=MESH))

    remote = []

    def send(source, target, sems, k, device):
        copy = pltpu.make_async_remote_copy(
            source, target, ssem.at[k] if sems is None else sems[0].at[k],
            rsem.at[k] if sems is None else sems[1].at[k], device_id=device, device_id_type=MESH,
        )
        copy.start()
        return copy

    w0 = [wts[pl.ds(home[plan[k]], 1), :] for k in range(4)]
    for k in range(4):
        wcur[4 + k] = jnp.broadcast_to(w0[k], (T, B))
    wcur[1] = wcur[5]
    wcur[2] = wcur[6]
    steps0 = [weight_steps(w0[2 * h], w0[2 * h + 1]) for h in range(2)]

    for load in loads:
        load.wait()
    r, c = iotas(B)
    eye, upper = r == c, r <= c
    for h in range(2):
        for k in range(2):
            praw[1 + h, :, B * k : B * (k + 1)] = xs[plan[2 * h + k]]
        hi, lo = split(praw[1 + h])
        ph[1 + h], plo[1 + h] = hi, lo
        gram = mm_t((hi, lo), (hi, lo))
        src0[pl.ds(2 * h * B, B)] = jnp.where(upper, gram[:B, :B], gram[B:, B:])
        src0[pl.ds((2 * h + 1) * B, B)] = gram[:B, B:]
        dsrc[h : h + 1] = diag_row(gram[B:, B:], eye)

    pl.semaphore_wait(barrier, N)

    def own(rows):
        return pl.ds(pl.multiple_of(rows * T, T), T)

    def scatter(k, source, target):
        peers_loop(me, lambda slot, p: send(source.at[own(p)], target.at[slot], None, k, (core, p)))

    def gather(k, target):
        peers_loop(me, lambda slot, p: send(target.at[own(me)], target.at[own(me)], None, k, (core, p)))

    def wait_all(sems, k, ref):
        pltpu.make_async_copy(ref, ref, sems.at[k]).wait()

    def most(ref):
        return ref.at[pl.ds(0, (N - 1) * T)]

    scatter(0, src0, rb0)
    peers_loop(me, lambda slot, p: send(dsrc, db0.at[slot], None, 1, (core, p)))
    d2d = [
        send(praw.at[1], praw.at[0], (dssem, drsem), 0, other),
        send(praw.at[2], praw.at[3], (dssem, drsem), 1, other),
        send(wcur.at[4], wcur.at[0], (dssem, drsem), 2, other),
        send(wcur.at[7], wcur.at[3], (dssem, drsem), 3, other),
    ]
    for copy in d2d:
        copy.wait_recv()
    for k in (0, 3):
        hi, lo = split(praw[k])
        ph[k], plo[k] = hi, lo
    order = [plan[4 + k] for k in range(4)]
    for h in range(2):
        i, j = order[2 * h], order[2 * h + 1]
        cross = mm_t((ph[i], plo[i]), (ph[j], plo[j]))
        srcx[h, 0:W] = cross[:, :B]
        srcx[h, W : 2 * W] = cross[:, B:]
    scatter(2, srcx.at[0], rbx.at[0])

    wait_all(rsem, 0, rb0)
    wait_all(rsem, 1, db0)
    g0[own(me)] = src0[own(me)] + jnp.sum(rb0[...], axis=0)
    gather(4, g0)
    scatter(3, srcx.at[1], rbx.at[1])
    d22 = dsrc[...] + jnp.sum(db0[...], axis=0)

    def cross_part(h):
        wait_all(rsem, 2 + h, rbx.at[h])
        gx[h, own(me)] = srcx[h, own(me)] + jnp.sum(rbx[h], axis=0)
        gather(5 + h, gx.at[h])

    cross_part(0)
    wait_all(rsem, 4, most(g0))
    gens = []
    for h in range(2):
        tri = g0[2 * h * B : (2 * h + 1) * B]
        a12 = g0[(2 * h + 1) * B : (2 * h + 2) * B]
        tri_t = tri.T
        a11 = jnp.where(upper, tri, tri_t)
        a22 = jnp.where(r > c, tri, jnp.where(eye, d22[h : h + 1], tri_t))
        gram = jnp.concatenate(
            [jnp.concatenate([a11, a12], axis=1), jnp.concatenate([a12.T, a22], axis=1)], axis=0
        )
        gfull[h] = gram
        gens.append(generator(gram, steps0[h]))
    q = newton_schulz(gens, (lambda: None, lambda: cross_part(1)))

    vsend[0], vbuf[1] = q[0][:, :B], q[0][:, B:]
    vbuf[2], vsend[1] = q[1][:, :B], q[1][:, B:]
    vcopies = [
        send(vsend.at[0], vbuf.at[0], (dssem, drsem), 4, other),
        send(vsend.at[1], vbuf.at[3], (dssem, drsem), 5, other),
    ]
    for h in range(2):
        qs = split(q[h])
        hq = split(mm(split(gfull[h]), qs))
        for k in range(2):
            cut = slice(B * k, B * (k + 1))
            block = mm_t(tuple(v[:, cut] for v in qs), tuple(v[:, cut] for v in hq))
            if h == k:
                gdsend[h] = block
            else:
                gd[1 + h] = block
    gcopies = [
        send(gdsend.at[0], gd.at[0], (dssem, drsem), 6, other),
        send(gdsend.at[1], gd.at[3], (dssem, drsem), 7, other),
    ]
    for copy in vcopies:
        copy.wait_recv()
    for h in range(2):
        wait_all(rsem, 5 + h, most(gx.at[h]))
    for k in range(4):
        rot[k] = mm((ph[k], plo[k]), split(vbuf[k]))
    crosses = []
    for h in range(2):
        i, j = order[2 * h], order[2 * h + 1]
        gxh = split(jnp.concatenate([gx[h, 0:W], gx[h, W : 2 * W]], axis=1))
        crosses.append(mm_t(split(vbuf[i]), split(mm(gxh, split(vbuf[j])))))
    for copy in gcopies:
        copy.wait_recv()
    gens = []
    for h in range(2):
        i, j = order[2 * h], order[2 * h + 1]
        gram = jnp.concatenate(
            [
                jnp.concatenate([gd[i], crosses[h]], axis=1),
                jnp.concatenate([crosses[h].T, gd[j]], axis=1),
            ],
            axis=0,
        )
        gfull[h] = gram
        gens.append(generator(gram, weight_steps(wcur[i, 0:1], wcur[j, 0:1])))
    q = newton_schulz(gens)

    stores = []
    for h in range(2):
        i, j = order[2 * h], order[2 * h + 1]
        qs = split(q[h])
        result = mm(split(jnp.concatenate([rot[i], rot[j]], axis=1)), qs)
        for k in range(2):
            obuf[2 * h + k] = result[:, B * k : B * (k + 1)]
            slot = 2 * h + k
            place = out.at[:, pl.ds(B * slot, B)]
            if slot in (0, 3):
                stores.append(send(obuf.at[slot], place, (dssem, drsem), 8 + k, other))
            else:
                copy = pltpu.make_async_copy(obuf.at[slot], place, osem.at[k])
                copy.start()
                stores.append(copy)
        squares = jnp.sum(q[h] * mm(split(gfull[h]), qs), axis=0, keepdims=True)
        root = jnp.sqrt(jnp.maximum(squares, 0.0))
        sent = root[:, h * B : (h + 1) * B]
        kept = root[:, (1 - h) * B : (2 - h) * B]
        nsend[h] = jnp.broadcast_to(sent, (T, B))
        stores.append(send(nsend.at[h], nrecv.at[h], (dssem, drsem), 10 + h, other))
        norms[1 + h : 2 + h] = kept
    for copy in stores:
        copy.wait()
    norms[0:1] = nrecv[0, 0:1]
    norms[3:4] = nrecv[1, 0:1]

    for copy in d2d + vcopies + gcopies:
        copy.wait_send()
    wait_all(ssem, 0, rb0)
    wait_all(ssem, 1, db0)
    for h in range(2):
        wait_all(ssem, 2 + h, rbx.at[h])
        wait_all(ssem, 5 + h, most(gx.at[h]))
    wait_all(ssem, 4, most(g0))


def body(snapshot, weights, block_home, plan):
    vmem = pl.BlockSpec(memory_space=pltpu.VMEM)
    smem = pl.BlockSpec(memory_space=pltpu.SMEM)
    anywhere = pl.BlockSpec(memory_space=pl.ANY)
    V, D = pltpu.VMEM, pltpu.SemaphoreType.DMA
    rotated, norms = pl.pallas_call(
        kernel,
        out_shape=(jax.ShapeDtypeStruct((ROWS, 4 * B), f32), jax.ShapeDtypeStruct((4, B), f32)),
        in_specs=[anywhere, vmem, smem, smem],
        out_specs=(anywhere, vmem),
        scratch_shapes=[
            V((4, ROWS, B), f32),
            V((4, ROWS, W), f32),
            V((4, ROWS, W), bf16),
            V((4, ROWS, W), bf16),
            V((8, T, B), f32),
            V((N * T, B), f32),
            V((2, B), f32),
            V((N - 1, T, B), f32),
            V((N - 1, 2, B), f32),
            V((2, N * T, B), f32),
            V((2, N - 1, T, B), f32),
            V((N * T, B), f32),
            V((2, N * T, B), f32),
            V((2, W, W), f32),
            V((4, W, B), f32),
            V((2, W, B), f32),
            V((4, B, B), f32),
            V((2, B, B), f32),
            V((4, ROWS, B), f32),
            V((4, ROWS, B), f32),
            V((2, T, B), f32),
            V((2, T, B), f32),
            D((4,)),
            D((2,)),
            D((7,)),
            D((7,)),
            D((12,)),
            D((12,)),
        ],
        compiler_params=pltpu.CompilerParams(
            collective_id=0, has_side_effects=True, vmem_limit_bytes=40 << 20
        ),
    )(snapshot, weights, block_home, plan.reshape(-1))
    return rotated, norms.reshape(-1)


def solution(mesh):
    in_specs = (P("row", "pair"), P(), P("pair"), P(None, "pair", None))
    out_specs = (P("row", "pair"), P("pair"))
    return jax.shard_map(body, mesh=mesh, in_specs=in_specs, out_specs=out_specs, check_vma=False)
```

time: 165 us -> 50.3 us (0.30)
  Pallas kernels: 0 us -> 45.1 us
  local copies, waits for them, and re-layouts: 46.7 us -> 3.73 us
  waiting for transfers between devices: 39.1 us -> 0 us
  starting transfers between devices: 34.8 us -> 0 us
  matrix products: 21.7 us -> 0 us
  blocking collectives: 16.8 us -> 0 us
  other arithmetic: 4.49 us -> 0.66 us
    pallas_call x0 -> x1, Pallas kernels: none -> 45.1 us  [body(): pl.pallas_call(kernel, out_shape=(jax.ShapeDtypeStruct((ROWS, 4 * B), f32...]
    all_to_all x4 -> x0, waiting for transfers between devices: 35.8 us -> none  [the longest x3 26.2 us: copy_for_each(): return lax.all_to_all(copies, axis, split_axis=0, concat_axis=0, tiled=True)]
    another operation x2 -> x0, local copies, waits for them, and re-layouts: 32.8 us -> none  [sum_by_parts(): return whole[:len(lines)].reshape(value.shape)]
    all_to_all x4 -> x0, starting transfers between devices: 26 us -> none  [the longest x3 14.1 us: copy_for_each(): return lax.all_to_all(copies, axis, split_axis=0, concat_axis=0, tiled=True)]
    dot_general x24 -> x0, matrix products: 21.7 us -> none  [the longest x10 10.8 us: rotation(): inner_gram = jnp.einsum('pcd,pce->pde', current, current, precision=highest)]
    all_to_all x1 -> x0, blocking collectives: 16.8 us -> none  [summed_on_arrival(): lax.all_to_all(split_up(value, dim, length), axis, 0, 0, tiled=True)]
    ppermute x6 -> x0, starting transfers between devices: 8.81 us -> none  [shifted(): return lax.ppermute(block, axis, route)]
    gather x7 -> x0, local copies, waits for them, and re-layouts: 7.48 us -> none  [the longest x2 4.64 us: rotation(): diagonal_part = jnp.diagonal(gram_matrix, axis1=1, axis2=2)]
  transfers between devices with their start and end apart: 10 -> 0, of which waited for: 10 -> 0; matrix products, arithmetic and copies ran while one was open for 3% -> 0% of each run, Pallas kernels for 0% -> 0%
where the time goes in v1:
time: 50.3 us; the launch traced here: 50.1 us
  Pallas kernels  45.1 us (90%)
  local copies, waits for them, and re-layouts  3.73 us (7%)
  between operations  0.67 us (1%)
  other arithmetic  0.66 us (1%)
    pallas_call x1, Pallas kernels, body(): pl.pallas_call(kernel, out_shape=(jax.ShapeDtypeStruct((ROWS, 4 * B), f32...  45.1 us
    unnamed x11, local copies, waits for them, and re-layouts  3.64 us

profile of v1, /device:TPU:1, one launch (start us, length us, event | category | flops | bytes accessed | tf_op | source)
XLA Modules:
  0.0 50.1 jit_solution(15995905993586981422)
XLA Ops:
  0.6 0.0 copy-start.3
  0.6 0.0 copy-start.1
  0.6 0.5 %broadcast.3 = s32[]{:T(128)} broadcast(s32[]{:T(128)} %constant.4), dimensions={} | broadcast | bytes 8 | tf_op args[3]
  1.2 0.1 copy-done.3
  1.3 0.7 %reduce.3 = s32[2,4]{1,0:T(2,128)S(1)} reduce(s32[2,1,4]{2,1,0:T(1,128)S(1)} %copy-done.3, s32[]{:T(128)} %broadcast.3), dimensions={1}, to_apply=%param.7.reduce_sub_computation.3 | reduce | bytes 68 | tf_op args[3]
  2.0 0.0 copy-start.2
  2.0 0.1 reshape.10.plan
  2.1 0.0 copy-done.1
  2.1 0.6 %copy-done.2 = s32[4]{0:T(128)S(1)} copy-done((s32[4]{0:T(128)S(1)}, s32[4]{0:T(128)}, u32[]{:S(2)}) %copy-start.2) | copy-done | bytes 40
  2.6 0.0 copy-start
  2.6 1.0 %copy-done = f32[256,512]{1,0:T(8,128)S(1)} copy-done((f32[256,512]{1,0:T(8,128)S(1)}, f32[256,512]{1,0:T(8,128)}, u32[]{:S(2)}) %copy-start) | copy-done | bytes 524312
  3.7 45.1 %shard_map.59 = (f32[256,512]{1,0:T(8,128)S(1)}, f32[4,128]{1,0:T(4,128)S(1)}) custom-call(f32[256,512]{1,0:T(8,128)S(1)} %copy-done, f32[8,128]{1,0:T(8,128)S(1)} %copy-done.1, s32[4]{0:T(128)S(1)} %copy-done.2, s32[8]{0:T(128)S(1)} %reshape.10.plan), custom_call_target="tpu_custom_call" | custom-call | tf_op jit(solution)/shard_map/pallas_call | solution.py:312
  48.7 0.8 %copy.8 = f32[256,512]{1,0:T(8,128)} copy(f32[256,512]{1,0:T(8,128)S(1)} %get-tuple-element.8) | data formatting | bytes 1048576
  49.5 0.6 %copy.9 = f32[512]{0:T(512)} copy(f32[512]{0:T(512)S(1)} %bitcast.1) | data formatting | bytes 4096
Async XLA Ops:
  0.6 0.7 %copy-start.3 = (s32[2,1,4]{2,1,0:T(1,128)S(1)}, s32[2,1,4]{2,1,0:T(1,128)}, u32[]{:S(2)}) copy-start(s32[2,1,4]{2,1,0:T(1,128)} %param.7) | copy-start | bytes 100
  0.6 1.4 %copy-start.1 = (f32[8,128]{1,0:T(8,128)S(1)}, f32[8,128]{1,0:T(8,128)}, u32[]{:S(2)}) copy-start(f32[8,128]{1,0:T(8,128)} %wts.1) | copy-start | bytes 12292
  2.0 0.7 %copy-start.2 = (s32[4]{0:T(128)S(1)}, s32[4]{0:T(128)}, u32[]{:S(2)}) copy-start(s32[4]{0:T(128)} %home.1) | copy-start | bytes 52
  2.6 1.0 %copy-start = (f32[256,512]{1,0:T(8,128)S(1)}, f32[256,512]{1,0:T(8,128)}, u32[]{:S(2)}) copy-start(f32[256,512]{1,0:T(8,128)} %snap.1) | copy-start | bytes 1572868

commit v2 on v1

--- a/solution.py
+++ b/solution.py
@@ -18,6 +18,10 @@
 N = SIDE**3
 T = 8
 FAR_FIRST = (2, 1, 3, 0)
+STRIDES = (1, SIDE, SIDE * SIDE)
+PLANE = SIDE * SIDE
+D = 2
+PARTS = ((24, 2), (24, 0), (16, 1))
 
 
 def split(x):
@@ -109,11 +113,33 @@
                     slot += 1
 
 
+def digit(me, d):
+    return lax.rem(me // STRIDES[d], SIDE)
+
+
+def plane_loop(me, line, send):
+    u, v = (d for d in range(3) if d != line)
+    mu, mv = digit(me, u), digit(me, v)
+    slot = 0
+    for a in FAR_FIRST:
+        for b in FAR_FIRST:
+            if a or b:
+                pu, pv = lax.rem(mu + a, SIDE), lax.rem(mv + b, SIDE)
+                send(slot, me + (pu - mu) * STRIDES[u] + (pv - mv) * STRIDES[v], pu * SIDE + pv)
+                slot += 1
+
+
+def plane_place(me, line):
+    u, v = (d for d in range(3) if d != line)
+    return digit(me, u) * SIDE + digit(me, v)
+
+
 def kernel(
     snap, wts, home, plan, out, norms,
-    xs, praw, ph, plo, wcur, src0, dsrc, rb0, db0, srcx, rbx, g0, gx, gfull, vbuf, vsend, gd, gdsend,
-    rot, obuf, nsend, nrecv, lsem, osem, ssem, rsem, dssem, drsem,
+    xs, praw, ph, plo, wcur, src0, rb0, srcx, rbx0, rbx1, rbx2, line0, line1, line2, g0, gx, gfull,
+    vbuf, vsend, gd, gdsend, rot, obuf, nsend, nrecv, lsem, osem, ssem, rsem, dssem, drsem,
 ):
+    rbx, lines = (rbx0, rbx1, rbx2), (line0, line1, line2)
     core, me = lax.axis_index("pair"), lax.axis_index("row")
     other = (1 - core, me)
     barrier = pltpu.get_barrier_semaphore()
@@ -133,7 +159,7 @@
         copy.start()
         return copy
 
-    w0 = [wts[pl.ds(home[plan[k]], 1), :] for k in range(4)]
+    w0 = [wts[pl.ds(home[plan[0, 0, k]], 1), :] for k in range(4)]
     for k in range(4):
         wcur[4 + k] = jnp.broadcast_to(w0[k], (T, B))
     wcur[1] = wcur[5]
@@ -146,33 +172,39 @@
     eye, upper = r == c, r <= c
     for h in range(2):
         for k in range(2):
-            praw[1 + h, :, B * k : B * (k + 1)] = xs[plan[2 * h + k]]
+            praw[1 + h, :, B * k : B * (k + 1)] = xs[plan[0, 0, 2 * h + k]]
         hi, lo = split(praw[1 + h])
         ph[1 + h], plo[1 + h] = hi, lo
         gram = mm_t((hi, lo), (hi, lo))
-        src0[pl.ds(2 * h * B, B)] = jnp.where(upper, gram[:B, :B], gram[B:, B:])
-        src0[pl.ds((2 * h + 1) * B, B)] = gram[:B, B:]
-        dsrc[h : h + 1] = diag_row(gram[B:, B:], eye)
+        packed = jnp.concatenate([jnp.where(upper, gram[:B, :B], gram[B:, B:]), gram[:B, B:]], axis=0)
+        src0[h * (N // 2) : (h + 1) * (N // 2), 0:T] = packed.reshape(N // 2, T, B)
+        src0[:, T + h : T + h + 1] = jnp.broadcast_to(diag_row(gram[B:, B:], eye), (N, 1, B))
 
     pl.semaphore_wait(barrier, N)
 
     def own(rows):
         return pl.ds(pl.multiple_of(rows * T, T), T)
 
-    def scatter(k, source, target):
-        peers_loop(me, lambda slot, p: send(source.at[own(p)], target.at[slot], None, k, (core, p)))
-
-    def gather(k, target):
-        peers_loop(me, lambda slot, p: send(target.at[own(me)], target.at[own(me)], None, k, (core, p)))
 
     def wait_all(sems, k, ref):
         pltpu.make_async_copy(ref, ref, sems.at[k]).wait()
 
-    def most(ref):
-        return ref.at[pl.ds(0, (N - 1) * T)]
-
-    scatter(0, src0, rb0)
-    peers_loop(me, lambda slot, p: send(dsrc, db0.at[slot], None, 1, (core, p)))
+    most0 = g0.at[pl.ds(0, (N - 1) * T)]
+    bases = (0, PARTS[0][0] * PLANE, (PARTS[0][0] + PARTS[1][0]) * PLANE)
+
+    def piece(part, place):
+        rows = PARTS[part][0]
+        return pl.ds(pl.multiple_of(bases[part] + place * rows, T), rows)
+
+    def most(part):
+        return gx.at[pl.ds(bases[part], (PLANE - 1) * PARTS[part][0])]
+
+    peers_loop(
+        me,
+        lambda slot, p: send(
+            src0.at[p, pl.ds(0, T + D)], rb0.at[slot, pl.ds(0, T + D)], None, 0, (core, p)
+        ),
+    )
     d2d = [
         send(praw.at[1], praw.at[0], (dssem, drsem), 0, other),
         send(praw.at[2], praw.at[3], (dssem, drsem), 1, other),
@@ -184,28 +216,47 @@
     for k in (0, 3):
         hi, lo = split(praw[k])
         ph[k], plo[k] = hi, lo
-    order = [plan[4 + k] for k in range(4)]
+    order = [plan[1, 0, k] for k in range(4)]
     for h in range(2):
         i, j = order[2 * h], order[2 * h + 1]
         cross = mm_t((ph[i], plo[i]), (ph[j], plo[j]))
-        srcx[h, 0:W] = cross[:, :B]
-        srcx[h, W : 2 * W] = cross[:, B:]
-    scatter(2, srcx.at[0], rbx.at[0])
-
-    wait_all(rsem, 0, rb0)
-    wait_all(rsem, 1, db0)
-    g0[own(me)] = src0[own(me)] + jnp.sum(rb0[...], axis=0)
-    gather(4, g0)
-    scatter(3, srcx.at[1], rbx.at[1])
-    d22 = dsrc[...] + jnp.sum(db0[...], axis=0)
-
-    def cross_part(h):
-        wait_all(rsem, 2 + h, rbx.at[h])
-        gx[h, own(me)] = srcx[h, own(me)] + jnp.sum(rbx[h], axis=0)
-        gather(5 + h, gx.at[h])
-
-    cross_part(0)
-    wait_all(rsem, 4, most(g0))
+        srcx[2 * h * W : (2 * h + 1) * W] = cross[:, :B]
+        srcx[(2 * h + 1) * W : (2 * h + 2) * W] = cross[:, B:]
+    for part, (rows, line) in enumerate(PARTS):
+        plane_loop(
+            me,
+            line,
+            lambda slot, p, place, part=part: send(
+                srcx.at[piece(part, place)], rbx[part].at[slot], None, 1 + part, (core, p)
+            ),
+        )
+
+    arrived = rb0.at[pl.ds(0, N - 1), pl.ds(0, T + D)]
+    wait_all(rsem, 0, arrived)
+    total = src0[me] + jnp.sum(rb0[...], axis=0)
+    g0[own(me)] = total[0:T]
+    peers_loop(me, lambda slot, p: send(g0.at[own(me)], g0.at[own(me)], None, 4, (core, p)))
+    d22 = total[T : T + D]
+
+    for part, (rows, line) in enumerate(PARTS):
+        wait_all(rsem, 1 + part, rbx[part])
+        mine = digit(me, line)
+        at_mine = lines[part].at[mine]
+        lines[part][mine] = srcx[piece(part, plane_place(me, line))] + jnp.sum(rbx[part][...], axis=0)
+        for a in range(1, SIDE):
+            p = me + (lax.rem(mine + a, SIDE) - mine) * STRIDES[line]
+            send(at_mine, at_mine, None, 5 + part, (core, p))
+
+    def cross_gather():
+        for part, (rows, line) in enumerate(PARTS):
+            wait_all(rsem, 5 + part, lines[part].at[pl.ds(0, SIDE - 1)])
+            here = piece(part, plane_place(me, line))
+            gx[here] = (lines[part][0] + lines[part][1]) + (lines[part][2] + lines[part][3])
+            plane_loop(
+                me, line, lambda slot, p, place, part=part: send(gx.at[here], gx.at[here], None, 8 + part, (core, p))
+            )
+
+    wait_all(rsem, 4, most0)
     gens = []
     for h in range(2):
         tri = g0[2 * h * B : (2 * h + 1) * B]
@@ -218,7 +269,7 @@
         )
         gfull[h] = gram
         gens.append(generator(gram, steps0[h]))
-    q = newton_schulz(gens, (lambda: None, lambda: cross_part(1)))
+    q = newton_schulz(gens, (cross_gather,))
 
     vsend[0], vbuf[1] = q[0][:, :B], q[0][:, B:]
     vbuf[2], vsend[1] = q[1][:, :B], q[1][:, B:]
@@ -242,14 +293,16 @@
     ]
     for copy in vcopies:
         copy.wait_recv()
-    for h in range(2):
-        wait_all(rsem, 5 + h, most(gx.at[h]))
+    for part in range(3):
+        wait_all(rsem, 8 + part, most(part))
     for k in range(4):
         rot[k] = mm((ph[k], plo[k]), split(vbuf[k]))
     crosses = []
     for h in range(2):
         i, j = order[2 * h], order[2 * h + 1]
-        gxh = split(jnp.concatenate([gx[h, 0:W], gx[h, W : 2 * W]], axis=1))
+        gxh = split(
+            jnp.concatenate([gx[2 * h * W : (2 * h + 1) * W], gx[(2 * h + 1) * W : (2 * h + 2) * W]], axis=1)
+        )
         crosses.append(mm_t(split(vbuf[i]), split(mm(gxh, split(vbuf[j])))))
     for copy in gcopies:
         copy.wait_recv()
@@ -296,19 +349,19 @@
 
     for copy in d2d + vcopies + gcopies:
         copy.wait_send()
-    wait_all(ssem, 0, rb0)
-    wait_all(ssem, 1, db0)
-    for h in range(2):
-        wait_all(ssem, 2 + h, rbx.at[h])
-        wait_all(ssem, 5 + h, most(gx.at[h]))
-    wait_all(ssem, 4, most(g0))
+    wait_all(ssem, 0, arrived)
+    wait_all(ssem, 4, most0)
+    for part in range(3):
+        wait_all(ssem, 1 + part, rbx[part])
+        wait_all(ssem, 5 + part, lines[part].at[pl.ds(0, SIDE - 1)])
+        wait_all(ssem, 8 + part, most(part))
 
 
 def body(snapshot, weights, block_home, plan):
     vmem = pl.BlockSpec(memory_space=pltpu.VMEM)
     smem = pl.BlockSpec(memory_space=pltpu.SMEM)
     anywhere = pl.BlockSpec(memory_space=pl.ANY)
-    V, D = pltpu.VMEM, pltpu.SemaphoreType.DMA
+    V, S = pltpu.VMEM, pltpu.SemaphoreType.DMA
     rotated, norms = pl.pallas_call(
         kernel,
         out_shape=(jax.ShapeDtypeStruct((ROWS, 4 * B), f32), jax.ShapeDtypeStruct((4, B), f32)),
@@ -320,14 +373,13 @@
             V((4, ROWS, W), bf16),
             V((4, ROWS, W), bf16),
             V((8, T, B), f32),
+            V((N, 2 * T, B), f32),
+            V((N - 1, 2 * T, B), f32),
+            V((4 * W, B), f32),
+            *[V((PLANE - 1, rows, B), f32) for rows, _ in PARTS],
+            *[V((SIDE, rows, B), f32) for rows, _ in PARTS],
             V((N * T, B), f32),
-            V((2, B), f32),
-            V((N - 1, T, B), f32),
-            V((N - 1, 2, B), f32),
-            V((2, N * T, B), f32),
-            V((2, N - 1, T, B), f32),
-            V((N * T, B), f32),
-            V((2, N * T, B), f32),
+            V((4 * W, B), f32),
             V((2, W, W), f32),
             V((4, W, B), f32),
             V((2, W, B), f32),
@@ -337,17 +389,17 @@
             V((4, ROWS, B), f32),
             V((2, T, B), f32),
             V((2, T, B), f32),
-            D((4,)),
-            D((2,)),
-            D((7,)),
-            D((7,)),
-            D((12,)),
-            D((12,)),
+            S((4,)),
+            S((2,)),
+            S((11,)),
+            S((11,)),
+            S((12,)),
+            S((12,)),
         ],
         compiler_params=pltpu.CompilerParams(
-            collective_id=0, has_side_effects=True, vmem_limit_bytes=40 << 20
+            collective_id=0, has_side_effects=True, vmem_limit_bytes=60 << 20
         ),
-    )(snapshot, weights, block_home, plan.reshape(-1))
+    )(snapshot, weights, block_home, plan)
     return rotated, norms.reshape(-1)
 
 

time: 50.3 us -> 46 us (0.915)
  Pallas kernels: 45.1 us -> 42.8 us
  local copies, waits for them, and re-layouts: 3.73 us -> 2.45 us
  other arithmetic: 0.66 us -> 0 us
    pallas_call x1, Pallas kernels: 45.1 us -> 42.8 us  [body(): pl.pallas_call(kernel, out_shape=(jax.ShapeDtypeStruct((ROWS, 4 * B), f32...]
    unnamed x11 -> x4, local copies, waits for them, and re-layouts: 3.64 us -> 2.45 us
    unnamed x1 -> x0, other arithmetic: 0.66 us -> none
where the time goes in v2:
time: 46 us; the launch traced here: 45.9 us
  Pallas kernels  42.8 us (93%)
  local copies, waits for them, and re-layouts  2.45 us (5%)
  between operations  0.65 us (1%)
    pallas_call x1, Pallas kernels, body(): pl.pallas_call(kernel, out_shape=(jax.ShapeDtypeStruct((ROWS, 4 * B), f32...  42.8 us
    unnamed x4, local copies, waits for them, and re-layouts  2.45 us

profile of v2, /device:TPU:1, one launch (start us, length us, event | category | flops | bytes accessed | tf_op | source)
XLA Modules:
  0.0 45.9 jit_solution(16057533221742520195)
XLA Ops:
  0.6 42.8 %shard_map.59 = (f32[256,512]{1,0:T(8,128)}, f32[4,128]{1,0:T(4,128)}) custom-call(f32[256,512]{1,0:T(8,128)} %snap.1, f32[8,128]{1,0:T(8,128)} %wts.1, s32[4]{0:T(128)} %home.1, s32[2,1,4]{2,1,0:T(1,128)} %plan.1), custom_call_target="tpu_custom_call" | custom-call | tf_op jit(solution)/shard_map/pallas_call | solution.py:365
  43.4 0.0 copy-start
  43.4 1.9 %copy.8 = f32[256,512]{1,0:T(8,128)} copy(f32[256,512]{1,0:T(8,128)} %get-tuple-element.8) | data formatting | bytes 1048576
  45.3 0.0 copy-done
  45.3 0.6 %copy.9 = f32[512]{0:T(512)} copy(f32[512]{0:T(512)S(1)} %bitcast.1) | data formatting | bytes 4096
Async XLA Ops:
  43.4 1.9 %copy-start = (f32[4,128]{1,0:T(4,128)S(1)}, f32[4,128]{1,0:T(4,128)}, u32[]{:S(2)}) copy-start(f32[4,128]{1,0:T(4,128)} %get-tuple-element.5) | copy-start | bytes 6148

commit v3 on v2

--- a/solution.py
+++ b/solution.py
@@ -37,9 +37,20 @@
     return lax.dot_general(a, b, (((0,), (0,)), ((), ())), preferred_element_type=f32)
 
 
+def halves(f, a):
+    cut = a.shape[0] // 2
+    return jnp.concatenate([f(a[:cut]), f(a[cut:])], axis=0)
+
+
 def mm(a, b):
     (ah, al), (bh, bl) = a, b
-    return dot(jnp.concatenate([ah, ah, al], axis=1), jnp.concatenate([bh, bl, bh], axis=0))
+    right = jnp.concatenate([bh, bl, bh], axis=0)
+    return halves(lambda left: dot(left, right), jnp.concatenate([ah, ah, al], axis=1))
+
+
+def mm1(a, b):
+    right = b.astype(bf16)
+    return halves(lambda left: dot(left, right), a.astype(bf16))
 
 
 def mm_t(a, b):
@@ -95,11 +106,9 @@
         z = [-0.75 * u[h] + 0.25 * mm(split(u[h]), zs[h]) for h in both]
         if k < len(between):
             between[k]()
-    zs = [split(z[h]) for h in both]
-    u = [mm(zs[h], zs[h]) for h in both]
-    tail = [split(0.375 * unit - 0.3125 * z[h] + 0.0625 * u[h]) for h in both]
-    last = [mm(split(u[h]), tail[h]) - 0.5 * z[h] for h in both]
-    return [x[h] + mm(split(x[h]), split(last[h])) for h in both]
+    u = [mm1(z[h], z[h]) for h in both]
+    last = [mm1(u[h], 0.375 * unit - 0.3125 * z[h] + 0.0625 * u[h]) - 0.5 * z[h] for h in both]
+    return x, last
 
 
 def peers_loop(me, send):
@@ -135,16 +144,20 @@
 
 
 def kernel(
-    snap, wts, home, plan, out, norms,
-    xs, praw, ph, plo, wcur, src0, rb0, srcx, rbx0, rbx1, rbx2, line0, line1, line2, g0, gx, gfull,
-    vbuf, vsend, gd, gdsend, rot, obuf, nsend, nrecv, lsem, osem, ssem, rsem, dssem, drsem,
+    snap, wts_in, home_in, plan_in, out, norms,
+    wts, home, plan, xs, praw, ph, plo, wcur, src0, rb0, srcx, rbx0, rbx1, rbx2, line0, line1, line2, g0, gx, gfull,
+    vbuf, vsend, gd, gdsend, rot, obuf, nsend, nrecv, lsem, ssem, rsem, dssem, drsem,
 ):
     rbx, lines = (rbx0, rbx1, rbx2), (line0, line1, line2)
     core, me = lax.axis_index("pair"), lax.axis_index("row")
     other = (1 - core, me)
     barrier = pltpu.get_barrier_semaphore()
     loads = [pltpu.make_async_copy(snap.at[:, pl.ds(B * s, B)], xs.at[s], lsem.at[s]) for s in range(4)]
-    for load in loads:
+    small = [
+        pltpu.make_async_copy(a, b, lsem.at[4 + k])
+        for k, (a, b) in enumerate(((wts_in, wts), (home_in, home), (plan_in, plan)))
+    ]
+    for load in small + loads:
         load.start()
     pl.semaphore_signal(barrier, inc=1, device_id=other, device_id_type=MESH)
     peers_loop(me, lambda slot, p: pl.semaphore_signal(barrier, inc=1, device_id=(core, p), device_id_type=MESH))
@@ -159,6 +172,8 @@
         copy.start()
         return copy
 
+    for load in small:
+        load.wait()
     w0 = [wts[pl.ds(home[plan[0, 0, k]], 1), :] for k in range(4)]
     for k in range(4):
         wcur[4 + k] = jnp.broadcast_to(w0[k], (T, B))
@@ -256,6 +271,7 @@
                 me, line, lambda slot, p, place, part=part: send(gx.at[here], gx.at[here], None, 8 + part, (core, p))
             )
 
+    cross_gather()
     wait_all(rsem, 4, most0)
     gens = []
     for h in range(2):
@@ -269,7 +285,10 @@
         )
         gfull[h] = gram
         gens.append(generator(gram, steps0[h]))
-    q = newton_schulz(gens, (cross_gather,))
+    x, last = newton_schulz(gens)
+    xs3, ls = [split(x[h]) for h in range(2)], [split(last[h]) for h in range(2)]
+    hx = [mm(split(gfull[h]), xs3[h]) for h in range(2)]
+    q = [x[h] + mm(xs3[h], ls[h]) for h in range(2)]
 
     vsend[0], vbuf[1] = q[0][:, :B], q[0][:, B:]
     vbuf[2], vsend[1] = q[1][:, :B], q[1][:, B:]
@@ -278,8 +297,8 @@
         send(vsend.at[1], vbuf.at[3], (dssem, drsem), 5, other),
     ]
     for h in range(2):
+        hq = split(hx[h] + mm(split(hx[h]), ls[h]))
         qs = split(q[h])
-        hq = split(mm(split(gfull[h]), qs))
         for k in range(2):
             cut = slice(B * k, B * (k + 1))
             block = mm_t(tuple(v[:, cut] for v in qs), tuple(v[:, cut] for v in hq))
@@ -291,12 +310,16 @@
         send(gdsend.at[0], gd.at[0], (dssem, drsem), 6, other),
         send(gdsend.at[1], gd.at[3], (dssem, drsem), 7, other),
     ]
+
+    def turn(k):
+        rot[k] = mm((ph[k], plo[k]), split(vbuf[k]))
+
+    turn(1)
+    turn(2)
     for copy in vcopies:
         copy.wait_recv()
     for part in range(3):
         wait_all(rsem, 8 + part, most(part))
-    for k in range(4):
-        rot[k] = mm((ph[k], plo[k]), split(vbuf[k]))
     crosses = []
     for h in range(2):
         i, j = order[2 * h], order[2 * h + 1]
@@ -318,30 +341,28 @@
         )
         gfull[h] = gram
         gens.append(generator(gram, weight_steps(wcur[i, 0:1], wcur[j, 0:1])))
-    q = newton_schulz(gens)
-
+
+    def turn_others():
+        turn(0)
+        turn(3)
+
+    x, last = newton_schulz(gens, (turn_others,))
     stores = []
     for h in range(2):
         i, j = order[2 * h], order[2 * h + 1]
-        qs = split(q[h])
-        result = mm(split(jnp.concatenate([rot[i], rot[j]], axis=1)), qs)
-        for k in range(2):
-            obuf[2 * h + k] = result[:, B * k : B * (k + 1)]
-            slot = 2 * h + k
-            place = out.at[:, pl.ds(B * slot, B)]
-            if slot in (0, 3):
-                stores.append(send(obuf.at[slot], place, (dssem, drsem), 8 + k, other))
-            else:
-                copy = pltpu.make_async_copy(obuf.at[slot], place, osem.at[k])
-                copy.start()
-                stores.append(copy)
-        squares = jnp.sum(q[h] * mm(split(gfull[h]), qs), axis=0, keepdims=True)
+        xs3, ls = split(x[h]), split(last[h])
+        rx = mm(split(jnp.concatenate([rot[i], rot[j]], axis=1)), xs3)
+        hx = mm(split(gfull[h]), xs3)
+        result = rx + mm(split(rx), ls)
+        obuf[h] = result[:, h * B : (h + 1) * B]
+        slot = 3 * h
+        stores.append(send(obuf.at[h], out.at[:, pl.ds(B * slot, B)], (dssem, drsem), 8 + h, other))
+        out[:, (1 + h) * B : (2 + h) * B] = result[:, (1 - h) * B : (2 - h) * B]
+        squares = jnp.sum((x[h] + mm(xs3, ls)) * (hx + mm(split(hx), ls)), axis=0, keepdims=True)
         root = jnp.sqrt(jnp.maximum(squares, 0.0))
-        sent = root[:, h * B : (h + 1) * B]
-        kept = root[:, (1 - h) * B : (2 - h) * B]
-        nsend[h] = jnp.broadcast_to(sent, (T, B))
+        nsend[h] = jnp.broadcast_to(root[:, h * B : (h + 1) * B], (T, B))
         stores.append(send(nsend.at[h], nrecv.at[h], (dssem, drsem), 10 + h, other))
-        norms[1 + h : 2 + h] = kept
+        norms[1 + h : 2 + h] = root[:, (1 - h) * B : (2 - h) * B]
     for copy in stores:
         copy.wait()
     norms[0:1] = nrecv[0, 0:1]
@@ -359,15 +380,17 @@
 
 def body(snapshot, weights, block_home, plan):
     vmem = pl.BlockSpec(memory_space=pltpu.VMEM)
-    smem = pl.BlockSpec(memory_space=pltpu.SMEM)
-    anywhere = pl.BlockSpec(memory_space=pl.ANY)
+    hbm = pl.BlockSpec(memory_space=pltpu.HBM)
     V, S = pltpu.VMEM, pltpu.SemaphoreType.DMA
     rotated, norms = pl.pallas_call(
         kernel,
         out_shape=(jax.ShapeDtypeStruct((ROWS, 4 * B), f32), jax.ShapeDtypeStruct((4, B), f32)),
-        in_specs=[anywhere, vmem, smem, smem],
-        out_specs=(anywhere, vmem),
+        in_specs=[hbm] * 4,
+        out_specs=(vmem, vmem),
         scratch_shapes=[
+            V((8, B), f32),
+            pltpu.SMEM((4,), jnp.int32),
+            pltpu.SMEM((2, 1, 4), jnp.int32),
             V((4, ROWS, B), f32),
             V((4, ROWS, W), f32),
             V((4, ROWS, W), bf16),
@@ -386,20 +409,19 @@
             V((4, B, B), f32),
             V((2, B, B), f32),
             V((4, ROWS, B), f32),
-            V((4, ROWS, B), f32),
+            V((2, ROWS, B), f32),
             V((2, T, B), f32),
             V((2, T, B), f32),
-            S((4,)),
-            S((2,)),
+            S((7,)),
             S((11,)),
             S((11,)),
             S((12,)),
             S((12,)),
         ],
         compiler_params=pltpu.CompilerParams(
-            collective_id=0, has_side_effects=True, vmem_limit_bytes=60 << 20
+            collective_id=0, has_side_effects=True, vmem_limit_bytes=32 << 20
         ),
-    )(snapshot, weights, block_home, plan)
+    )(*[pltpu.with_memory_space_constraint(a, pltpu.HBM) for a in (snapshot, weights, block_home, plan)])
     return rotated, norms.reshape(-1)
 
 

time: 46 us -> 41.4 us (0.900)
  Pallas kernels: 42.8 us -> 39.3 us
  local copies, waits for them, and re-layouts: 2.45 us -> 1.37 us
    pallas_call x1, Pallas kernels: 42.8 us -> 39.3 us  [body(): pl.pallas_call(kernel, out_shape=(jax.ShapeDtypeStruct((ROWS, 4 * B), f32...]
    unnamed x4 -> x2, local copies, waits for them, and re-layouts: 2.45 us -> 1.37 us
where the time goes in v3:
time: 41.4 us; the launch traced here: 41.3 us
  Pallas kernels  39.3 us (95%)
  local copies, waits for them, and re-layouts  1.37 us (3%)
  between operations  0.64 us (2%)
    pallas_call x1, Pallas kernels, body(): pl.pallas_call(kernel, out_shape=(jax.ShapeDtypeStruct((ROWS, 4 * B), f32...  39.3 us
    unnamed x2, local copies, waits for them, and re-layouts  1.37 us

profile of v3, /device:TPU:1, one launch (start us, length us, event | category | flops | bytes accessed | tf_op | source)
XLA Modules:
  0.0 41.3 jit_solution(4669170404759079251)
XLA Ops:
  0.6 39.3 %shard_map.59 = (f32[256,512]{1,0:T(8,128)S(1)}, f32[4,128]{1,0:T(4,128)S(1)}) custom-call(f32[256,512]{1,0:T(8,128)} %snap.1, f32[8,128]{1,0:T(8,128)} %wts_in.1, s32[4]{0:T(128)} %home_in.1, s32[2,1,4]{2,1,0:T(1,128)} %plan_in.1), custom_call_target="tpu_custom_call" | custom-call | tf_op jit(solution)/shard_map/pallas_call | solution.py:385
  39.9 0.8 %copy.8 = f32[256,512]{1,0:T(8,128)} copy(f32[256,512]{1,0:T(8,128)S(1)} %get-tuple-element.8) | data formatting | bytes 1048576
  40.7 0.6 %copy.9 = f32[512]{0:T(512)} copy(f32[512]{0:T(512)S(1)} %bitcast.1) | data formatting | bytes 4096

commit v4 on v3

--- a/solution.py
+++ b/solution.py
@@ -33,10 +33,6 @@
     return jnp.dot(a, b, preferred_element_type=f32)
 
 
-def dot_t(a, b):
-    return lax.dot_general(a, b, (((0,), (0,)), ((), ())), preferred_element_type=f32)
-
-
 def halves(f, a):
     cut = a.shape[0] // 2
     return jnp.concatenate([f(a[:cut]), f(a[cut:])], axis=0)
@@ -53,9 +49,18 @@
     return halves(lambda left: dot(left, right), a.astype(bf16))
 
 
-def mm_t(a, b):
-    (ah, al), (bh, bl) = a, b
-    return dot_t(jnp.concatenate([ah, ah, al], axis=0), jnp.concatenate([bh, bl, bh], axis=0))
+def split3(x):
+    hi, rest = x.astype(bf16), x
+    rest = rest - hi.astype(f32)
+    mid = rest.astype(bf16)
+    return hi, mid, (rest - mid.astype(f32)).astype(bf16)
+
+
+def mm6(a, b):
+    (ah, am, al), (bh, bm, bl) = a, b
+    right = jnp.concatenate([bh, bm, bh, bm, bl, bh], axis=0)
+    left = jnp.concatenate([ah, ah, am, am, ah, al], axis=1)
+    return halves(lambda rows: dot(rows, right), left)
 
 
 def iotas(n):
@@ -111,14 +116,17 @@
     return x, last
 
 
-def peers_loop(me, send):
-    z, y, x = me // (SIDE * SIDE), lax.rem(me // SIDE, SIDE), lax.rem(me, SIDE)
+def ring_digits(me):
+    return [[lax.rem(me // stride + a, SIDE) * stride for a in range(SIDE)] for stride in STRIDES]
+
+
+def peers_loop(terms, send):
     slot = 0
     for a in FAR_FIRST:
         for b in FAR_FIRST:
             for c in FAR_FIRST:
                 if a or b or c:
-                    send(slot, lax.rem(z + a, SIDE) * SIDE * SIDE + lax.rem(y + b, SIDE) * SIDE + lax.rem(x + c, SIDE))
+                    send(slot, terms[2][a] + terms[1][b] + terms[0][c])
                     slot += 1
 
 
@@ -126,16 +134,21 @@
     return lax.rem(me // STRIDES[d], SIDE)
 
 
-def plane_loop(me, line, send):
+def plane_loop(terms, line, send):
     u, v = (d for d in range(3) if d != line)
-    mu, mv = digit(me, u), digit(me, v)
     slot = 0
     for a in FAR_FIRST:
         for b in FAR_FIRST:
             if a or b:
-                pu, pv = lax.rem(mu + a, SIDE), lax.rem(mv + b, SIDE)
-                send(slot, me + (pu - mu) * STRIDES[u] + (pv - mv) * STRIDES[v], pu * SIDE + pv)
+                pu, pv = terms[u][a], terms[v][b]
+                place = pu // STRIDES[u] * SIDE + pv // STRIDES[v]
+                send(slot, terms[line][0] + pu + pv, place)
                 slot += 1
+
+
+def short_sum(blocks, groups):
+    parts = [functools.reduce(lambda a, b: a + b, blocks[k::groups]) for k in range(groups)]
+    return functools.reduce(lambda a, b: a + b, parts)
 
 
 def plane_place(me, line):
@@ -145,12 +158,13 @@
 
 def kernel(
     snap, wts_in, home_in, plan_in, out, norms,
-    wts, home, plan, xs, praw, ph, plo, wcur, src0, rb0, srcx, rbx0, rbx1, rbx2, line0, line1, line2, g0, gx, gfull,
+    wts, home, plan, xs, praw, wcur, src0, rb0, srcx, rbx0, rbx1, rbx2, line0, line1, line2, g0, gx, gfull,
     vbuf, vsend, gd, gdsend, rot, obuf, nsend, nrecv, lsem, ssem, rsem, dssem, drsem,
 ):
     rbx, lines = (rbx0, rbx1, rbx2), (line0, line1, line2)
     core, me = lax.axis_index("pair"), lax.axis_index("row")
     other = (1 - core, me)
+    terms = ring_digits(me)
     barrier = pltpu.get_barrier_semaphore()
     loads = [pltpu.make_async_copy(snap.at[:, pl.ds(B * s, B)], xs.at[s], lsem.at[s]) for s in range(4)]
     small = [
@@ -160,7 +174,7 @@
     for load in small + loads:
         load.start()
     pl.semaphore_signal(barrier, inc=1, device_id=other, device_id_type=MESH)
-    peers_loop(me, lambda slot, p: pl.semaphore_signal(barrier, inc=1, device_id=(core, p), device_id_type=MESH))
+    peers_loop(terms, lambda slot, p: pl.semaphore_signal(barrier, inc=1, device_id=(core, p), device_id_type=MESH))
 
     remote = []
 
@@ -188,76 +202,74 @@
     for h in range(2):
         for k in range(2):
             praw[1 + h, :, B * k : B * (k + 1)] = xs[plan[0, 0, 2 * h + k]]
-        hi, lo = split(praw[1 + h])
-        ph[1 + h], plo[1 + h] = hi, lo
-        gram = mm_t((hi, lo), (hi, lo))
-        packed = jnp.concatenate([jnp.where(upper, gram[:B, :B], gram[B:, B:]), gram[:B, B:]], axis=0)
-        src0[h * (N // 2) : (h + 1) * (N // 2), 0:T] = packed.reshape(N // 2, T, B)
-        src0[:, T + h : T + h + 1] = jnp.broadcast_to(diag_row(gram[B:, B:], eye), (N, 1, B))
 
     pl.semaphore_wait(barrier, N)
-
-    def own(rows):
-        return pl.ds(pl.multiple_of(rows * T, T), T)
-
-
-    def wait_all(sems, k, ref):
-        pltpu.make_async_copy(ref, ref, sems.at[k]).wait()
-
-    most0 = g0.at[pl.ds(0, (N - 1) * T)]
-    bases = (0, PARTS[0][0] * PLANE, (PARTS[0][0] + PARTS[1][0]) * PLANE)
-
-    def piece(part, place):
-        rows = PARTS[part][0]
-        return pl.ds(pl.multiple_of(bases[part] + place * rows, T), rows)
-
-    def most(part):
-        return gx.at[pl.ds(bases[part], (PLANE - 1) * PARTS[part][0])]
-
-    peers_loop(
-        me,
-        lambda slot, p: send(
-            src0.at[p, pl.ds(0, T + D)], rb0.at[slot, pl.ds(0, T + D)], None, 0, (core, p)
-        ),
-    )
     d2d = [
         send(praw.at[1], praw.at[0], (dssem, drsem), 0, other),
         send(praw.at[2], praw.at[3], (dssem, drsem), 1, other),
         send(wcur.at[4], wcur.at[0], (dssem, drsem), 2, other),
         send(wcur.at[7], wcur.at[3], (dssem, drsem), 3, other),
     ]
+    for h in range(2):
+        pair = praw[1 + h]
+        gram = mm6(split3(pair.T), split3(pair))
+        packed = jnp.concatenate([jnp.where(upper, gram[:B, :B], gram[B:, B:]), gram[:B, B:]], axis=0)
+        src0[h * (N // 2) : (h + 1) * (N // 2), 0:T] = packed.reshape(N // 2, T, B)
+        src0[:, T + h : T + h + 1] = jnp.broadcast_to(diag_row(gram[B:, B:], eye), (N, 1, B))
+
+    def own(rows):
+        return pl.ds(pl.multiple_of(rows * T, T), T)
+
+
+    def wait_all(sems, k, ref):
+        pltpu.make_async_copy(ref, ref, sems.at[k]).wait()
+
+    most0 = g0.at[pl.ds(0, (N - 1) * T)]
+    bases = (0, PARTS[0][0] * PLANE, (PARTS[0][0] + PARTS[1][0]) * PLANE)
+
+    def piece(part, place):
+        rows = PARTS[part][0]
+        return pl.ds(pl.multiple_of(bases[part] + place * rows, T), rows)
+
+    def most(part):
+        return gx.at[pl.ds(bases[part], (PLANE - 1) * PARTS[part][0])]
+
+    peers_loop(
+        terms,
+        lambda slot, p: send(
+            src0.at[p, pl.ds(0, T + D)], rb0.at[slot, pl.ds(0, T + D)], None, 0, (core, p)
+        ),
+    )
     for copy in d2d:
         copy.wait_recv()
-    for k in (0, 3):
-        hi, lo = split(praw[k])
-        ph[k], plo[k] = hi, lo
     order = [plan[1, 0, k] for k in range(4)]
     for h in range(2):
         i, j = order[2 * h], order[2 * h + 1]
-        cross = mm_t((ph[i], plo[i]), (ph[j], plo[j]))
+        cross = mm6(split3(praw[i].T), split3(praw[j]))
         srcx[2 * h * W : (2 * h + 1) * W] = cross[:, :B]
         srcx[(2 * h + 1) * W : (2 * h + 2) * W] = cross[:, B:]
     for part, (rows, line) in enumerate(PARTS):
         plane_loop(
-            me,
+            terms,
             line,
             lambda slot, p, place, part=part: send(
                 srcx.at[piece(part, place)], rbx[part].at[slot], None, 1 + part, (core, p)
             ),
         )
 
+    steps1 = [weight_steps(wcur[order[2 * h], 0:1], wcur[order[2 * h + 1], 0:1]) for h in range(2)]
     arrived = rb0.at[pl.ds(0, N - 1), pl.ds(0, T + D)]
     wait_all(rsem, 0, arrived)
-    total = src0[me] + jnp.sum(rb0[...], axis=0)
+    total = src0[me] + short_sum([rb0[k] for k in range(N - 1)], 9)
     g0[own(me)] = total[0:T]
-    peers_loop(me, lambda slot, p: send(g0.at[own(me)], g0.at[own(me)], None, 4, (core, p)))
+    peers_loop(terms, lambda slot, p: send(g0.at[own(me)], g0.at[own(me)], None, 4, (core, p)))
     d22 = total[T : T + D]
 
     for part, (rows, line) in enumerate(PARTS):
         wait_all(rsem, 1 + part, rbx[part])
         mine = digit(me, line)
         at_mine = lines[part].at[mine]
-        lines[part][mine] = srcx[piece(part, plane_place(me, line))] + jnp.sum(rbx[part][...], axis=0)
+        lines[part][mine] = srcx[piece(part, plane_place(me, line))] + short_sum([rbx[part][k] for k in range(PLANE - 1)], 3)
         for a in range(1, SIDE):
             p = me + (lax.rem(mine + a, SIDE) - mine) * STRIDES[line]
             send(at_mine, at_mine, None, 5 + part, (core, p))
@@ -268,7 +280,7 @@
             here = piece(part, plane_place(me, line))
             gx[here] = (lines[part][0] + lines[part][1]) + (lines[part][2] + lines[part][3])
             plane_loop(
-                me, line, lambda slot, p, place, part=part: send(gx.at[here], gx.at[here], None, 8 + part, (core, p))
+                terms, line, lambda slot, p, place, part=part: send(gx.at[here], gx.at[here], None, 8 + part, (core, p))
             )
 
     cross_gather()
@@ -287,7 +299,7 @@
         gens.append(generator(gram, steps0[h]))
     x, last = newton_schulz(gens)
     xs3, ls = [split(x[h]) for h in range(2)], [split(last[h]) for h in range(2)]
-    hx = [mm(split(gfull[h]), xs3[h]) for h in range(2)]
+    hx = [mm6(split3(gfull[h]), split3(x[h])) for h in range(2)]
     q = [x[h] + mm(xs3[h], ls[h]) for h in range(2)]
 
     vsend[0], vbuf[1] = q[0][:, :B], q[0][:, B:]
@@ -297,11 +309,11 @@
         send(vsend.at[1], vbuf.at[3], (dssem, drsem), 5, other),
     ]
     for h in range(2):
-        hq = split(hx[h] + mm(split(hx[h]), ls[h]))
-        qs = split(q[h])
+        hq = split3(hx[h] + mm(split(hx[h]), ls[h]))
+        qt = split3(q[h].T)
         for k in range(2):
             cut = slice(B * k, B * (k + 1))
-            block = mm_t(tuple(v[:, cut] for v in qs), tuple(v[:, cut] for v in hq))
+            block = mm6(tuple(v[cut] for v in qt), tuple(v[:, cut] for v in hq))
             if h == k:
                 gdsend[h] = block
             else:
@@ -312,10 +324,8 @@
     ]
 
     def turn(k):
-        rot[k] = mm((ph[k], plo[k]), split(vbuf[k]))
-
-    turn(1)
-    turn(2)
+        rot[k] = mm(split(praw[k]), split(vbuf[k]))
+
     for copy in vcopies:
         copy.wait_recv()
     for part in range(3):
@@ -323,10 +333,10 @@
     crosses = []
     for h in range(2):
         i, j = order[2 * h], order[2 * h + 1]
-        gxh = split(
+        gxh = split3(
             jnp.concatenate([gx[2 * h * W : (2 * h + 1) * W], gx[(2 * h + 1) * W : (2 * h + 2) * W]], axis=1)
         )
-        crosses.append(mm_t(split(vbuf[i]), split(mm(gxh, split(vbuf[j])))))
+        crosses.append(mm6(split3(vbuf[i].T), split3(mm6(gxh, split3(vbuf[j])))))
     for copy in gcopies:
         copy.wait_recv()
     gens = []
@@ -340,29 +350,34 @@
             axis=0,
         )
         gfull[h] = gram
-        gens.append(generator(gram, weight_steps(wcur[i, 0:1], wcur[j, 0:1])))
-
-    def turn_others():
-        turn(0)
-        turn(3)
-
-    x, last = newton_schulz(gens, (turn_others,))
+        gens.append(generator(gram, steps1[h]))
+
+    def turn_all():
+        for k in range(4):
+            turn(k)
+
+    x, last = newton_schulz(gens, (turn_all,))
+    both = range(2)
+    xs3, ls = [split(x[h]) for h in both], [split(last[h]) for h in both]
+    rx = [
+        mm(split(jnp.concatenate([rot[order[2 * h]], rot[order[2 * h + 1]]], axis=1)), xs3[h]) for h in both
+    ]
+    hx = [mm(split(gfull[h]), xs3[h]) for h in both]
+    result = [rx[h] + mm(split(rx[h]), ls[h]) for h in both]
     stores = []
-    for h in range(2):
-        i, j = order[2 * h], order[2 * h + 1]
-        xs3, ls = split(x[h]), split(last[h])
-        rx = mm(split(jnp.concatenate([rot[i], rot[j]], axis=1)), xs3)
-        hx = mm(split(gfull[h]), xs3)
-        result = rx + mm(split(rx), ls)
-        obuf[h] = result[:, h * B : (h + 1) * B]
-        slot = 3 * h
-        stores.append(send(obuf.at[h], out.at[:, pl.ds(B * slot, B)], (dssem, drsem), 8 + h, other))
-        out[:, (1 + h) * B : (2 + h) * B] = result[:, (1 - h) * B : (2 - h) * B]
-        squares = jnp.sum((x[h] + mm(xs3, ls)) * (hx + mm(split(hx), ls)), axis=0, keepdims=True)
-        root = jnp.sqrt(jnp.maximum(squares, 0.0))
-        nsend[h] = jnp.broadcast_to(root[:, h * B : (h + 1) * B], (T, B))
+    for h in both:
+        obuf[h] = result[h][:, h * B : (h + 1) * B]
+        place = out.at[:, pl.ds(3 * h * B, B)]
+        stores.append(send(obuf.at[h], place, (dssem, drsem), 8 + h, other))
+    root = []
+    for h in both:
+        squares = jnp.sum((x[h] + mm(xs3[h], ls[h])) * (hx[h] + mm(split(hx[h]), ls[h])), axis=0, keepdims=True)
+        root.append(jnp.sqrt(jnp.maximum(squares, 0.0)))
+        nsend[h] = jnp.broadcast_to(root[h][:, h * B : (h + 1) * B], (T, B))
         stores.append(send(nsend.at[h], nrecv.at[h], (dssem, drsem), 10 + h, other))
-        norms[1 + h : 2 + h] = root[:, (1 - h) * B : (2 - h) * B]
+    for h in both:
+        out[:, (1 + h) * B : (2 + h) * B] = result[h][:, (1 - h) * B : (2 - h) * B]
+        norms[1 + h : 2 + h] = root[h][:, (1 - h) * B : (2 - h) * B]
     for copy in stores:
         copy.wait()
     norms[0:1] = nrecv[0, 0:1]
@@ -393,8 +408,6 @@
             pltpu.SMEM((2, 1, 4), jnp.int32),
             V((4, ROWS, B), f32),
             V((4, ROWS, W), f32),
-            V((4, ROWS, W), bf16),
-            V((4, ROWS, W), bf16),
             V((8, T, B), f32),
             V((N, 2 * T, B), f32),
             V((N - 1, 2 * T, B), f32),

time: 41.4 us -> 41.7 us (level)
  no operation moved by 1% of the time
where the time goes in v4:
time: 41.7 us; the launch traced here: 41.6 us
  Pallas kernels  39.6 us (95%)
  local copies, waits for them, and re-layouts  1.37 us (3%)
  between operations  0.64 us (2%)
    pallas_call x1, Pallas kernels, body(): pl.pallas_call(kernel, out_shape=(jax.ShapeDtypeStruct((ROWS, 4 * B), f32...  39.6 us
    unnamed x2, local copies, waits for them, and re-layouts  1.37 us

profile of v4, /device:TPU:1, one launch (start us, length us, event | category | flops | bytes accessed | tf_op | source)
XLA Modules:
  0.0 41.6 jit_solution(8786709093518475241)
XLA Ops:
  0.6 39.6 %shard_map.59 = (f32[256,512]{1,0:T(8,128)S(1)}, f32[4,128]{1,0:T(4,128)S(1)}) custom-call(f32[256,512]{1,0:T(8,128)} %snap.1, f32[8,128]{1,0:T(8,128)} %wts_in.1, s32[4]{0:T(128)} %home_in.1, s32[2,1,4]{2,1,0:T(1,128)} %plan_in.1), custom_call_target="tpu_custom_call" | custom-call | tf_op jit(solution)/shard_map/pallas_call | solution.py:400
  40.2 0.8 %copy.8 = f32[256,512]{1,0:T(8,128)} copy(f32[256,512]{1,0:T(8,128)S(1)} %get-tuple-element.8) | data formatting | bytes 1048576
  41.0 0.6 %copy.9 = f32[512]{0:T(512)} copy(f32[512]{0:T(512)S(1)} %bitcast.1) | data formatting | bytes 4096

commit v5 on v4

--- a/solution.py
+++ b/solution.py
@@ -326,6 +326,8 @@
     def turn(k):
         rot[k] = mm(split(praw[k]), split(vbuf[k]))
 
+    turn(1)
+    turn(2)
     for copy in vcopies:
         copy.wait_recv()
     for part in range(3):
@@ -353,7 +355,7 @@
         gens.append(generator(gram, steps1[h]))
 
     def turn_all():
-        for k in range(4):
+        for k in (0, 3):
             turn(k)
 
     x, last = newton_schulz(gens, (turn_all,))

time: 41.7 us -> 41.5 us (level)
  no operation moved by 1% of the time
where the time goes in v5:
time: 41.5 us; the launch traced here: 41.4 us
  Pallas kernels  39.4 us (95%)
  local copies, waits for them, and re-layouts  1.37 us (3%)
  between operations  0.64 us (2%)
    pallas_call x1, Pallas kernels, body(): pl.pallas_call(kernel, out_shape=(jax.ShapeDtypeStruct((ROWS, 4 * B), f32...  39.4 us
    unnamed x2, local copies, waits for them, and re-layouts  1.37 us

profile of v5, /device:TPU:1, one launch (start us, length us, event | category | flops | bytes accessed | tf_op | source)
XLA Modules:
  0.0 41.4 jit_solution(4606778577221167989)
XLA Ops:
  0.6 39.4 %shard_map.59 = (f32[256,512]{1,0:T(8,128)S(1)}, f32[4,128]{1,0:T(4,128)S(1)}) custom-call(f32[256,512]{1,0:T(8,128)} %snap.1, f32[8,128]{1,0:T(8,128)} %wts_in.1, s32[4]{0:T(128)} %home_in.1, s32[2,1,4]{2,1,0:T(1,128)} %plan_in.1), custom_call_target="tpu_custom_call" | custom-call | tf_op jit(solution)/shard_map/pallas_call | solution.py:402
  40.0 0.8 %copy.8 = f32[256,512]{1,0:T(8,128)} copy(f32[256,512]{1,0:T(8,128)S(1)} %get-tuple-element.8) | data formatting | bytes 1048576
  40.8 0.6 %copy.9 = f32[512]{0:T(512)} copy(f32[512]{0:T(512)S(1)} %bitcast.1) | data formatting | bytes 4096
